TPU v7x, 32 devices: a whole 2x2x4 slice. The times are simulated.
32 devices in a mesh: ep: 8 (over z, x), tp: 4 (over y, core).
Axes of the slice: x: 2, y: 2, z: 4, core: 2. Of those that a mesh axis runs over, the one named last changes fastest.
Arguments:
- hidden_in: bfloat16 [1024, 2048], P('ep', 'tp'), may hold values from -6 to 6
- norm_gain: float32 [2048], replicated, may hold values from 0.5 to 1.5
- router_weight: bfloat16 [2048, 8], replicated, may hold values from -4.861359 to 4.861359
- shared_gate_up: bfloat16 [2048, 2, 1408], P(None, None, 'tp'), may hold values from -0.125 to 0.125
- shared_down: bfloat16 [1408, 2048], P('tp'), may hold values from -0.15625 to 0.15625
- slot_gate_up: bfloat16 [32, 2048, 2, 704], P(('ep', 'tp')), as said below
- slot_down: bfloat16 [32, 704, 2048], P(('ep', 'tp')), as said below
- slot_expert: int32 [32], replicated, may hold values from 0 to 7, as said below
- slot_choice: int32 [1024, 6], P('ep'), may hold values from 0 to 31, all different within a row; in each aligned block of 32 rows (0 to 31, 32 to 63, ...) at most 12 rows name the same one
- live_count: int32 [8], P('ep'), may hold values from 64 to 128, as said below
Outputs:
- mixed_out: bfloat16 [1024, 2048], P('ep', 'tp')
Inputs may be any that keep to these rules, and one draw needn't show every extreme that they name: `slot_expert`: each expert is held by 1 or 7 slots; exactly 4 experts by the larger number. `slot_gate_up`: entry s holds the weights of expert slot_expert[s]; slots of one expert hold equal weights. `slot_down`: entry s holds the weights of expert slot_expert[s]; slots of one expert hold equal weights. `slot_choice`: a row names 6 different slots; in each aligned block of 32 rows no slot is named more than 12 times. `live_count`: the live rows of an index of ep are its first ones; some index of ep has all 128 rows live.
All inputs are finite; a program needn't handle non-finite values.
Results may differ from a plain program's by a relative error of at most 0.0058.
Values may be sent and summed in bfloat16 or wider, within the bound.
A program may use at most 64 MiB of HBM per device.

v0:
```python
import jax
import jax.numpy as jnp
from jax import lax
from jax.sharding import PartitionSpec as P


def gate_weights(normed_rows, choices, router_weight, slot_expert):
    logits = jnp.dot(normed_rows, router_weight, preferred_element_type=jnp.float32)
    slot_total = slot_expert.shape[0]
    expert_total = router_weight.shape[1]
    slot_hit = choices[:, :, None] == jnp.arange(slot_total, dtype=jnp.int32)
    expert_ids = jnp.sum(jnp.where(slot_hit, slot_expert, 0), axis=2)
    expert_hit = expert_ids[:, :, None] == jnp.arange(expert_total, dtype=jnp.int32)
    picked = jnp.sum(jnp.where(expert_hit, logits[:, None, :], 0.0), axis=2)
    highest = jnp.max(picked, axis=1, keepdims=True)
    weights = jnp.exp(picked - highest)
    return (weights / jnp.sum(weights, axis=1, keepdims=True)).astype(jnp.bfloat16)


def slot_positions(targets):
    length = targets.shape[0]
    same_slot = targets[:, None] == targets[None, :]
    earlier = jnp.arange(length)[None, :] < jnp.arange(length)[:, None]
    return jnp.sum(same_slot & earlier, axis=1)


def expert_apply(received, slot_gate_up, slot_down):
    shape_in = received.shape
    flat_rows = received.reshape(-1, shape_in[-1])
    gate_up = jnp.einsum(
        "rd,dgf->rgf", flat_rows, slot_gate_up[0], preferred_element_type=jnp.float32
    )
    activated = (jax.nn.silu(gate_up[:, 0]) * gate_up[:, 1]).astype(jnp.bfloat16)
    result = jnp.dot(activated, slot_down[0], preferred_element_type=jnp.float32).astype(
        jnp.bfloat16
    )
    return result.reshape(shape_in)


def local(
    hidden_in,
    norm_gain,
    router_weight,
    shared_gate_up,
    shared_down,
    slot_gate_up,
    slot_down,
    slot_expert,
    slot_choice,
    live_count,
):
    tp_count = lax.axis_size("tp")
    ep_count = lax.axis_size("ep")
    tp_index = lax.axis_index("tp")
    tok_count = hidden_in.shape[0]
    feature_width = hidden_in.shape[1] * tp_count
    top_count = slot_choice.shape[1]
    slot_count = slot_expert.shape[0]
    quarter = tok_count // tp_count
    capacity = max(2, 2 * quarter * top_count // slot_count)
    full_rows = lax.all_gather(hidden_in, "tp", axis=1, tiled=True)
    wide_rows = full_rows.astype(jnp.float32)
    norm_scale = lax.rsqrt(jnp.mean(wide_rows * wide_rows, axis=1, keepdims=True) + 1e-06)
    normed = (wide_rows * norm_scale * norm_gain).astype(jnp.bfloat16)
    shared_proj = jnp.einsum(
        "td,dgf->tgf", normed, shared_gate_up, preferred_element_type=jnp.float32
    )
    shared_hidden = (jax.nn.silu(shared_proj[:, 0]) * shared_proj[:, 1]).astype(jnp.bfloat16)
    partial_value = jnp.dot(shared_hidden, shared_down, preferred_element_type=jnp.float32)
    row_start = tp_index * quarter
    own_rows = lax.dynamic_slice_in_dim(normed, row_start, quarter, 0)
    own_choice = lax.dynamic_slice_in_dim(slot_choice, row_start, quarter, 0)
    gate_values = gate_weights(own_rows, own_choice, router_weight, slot_expert)
    targets = own_choice.reshape(-1)
    placed = targets * capacity + slot_positions(targets)
    outgoing = jnp.zeros((slot_count * capacity, feature_width), jnp.bfloat16)
    outgoing = outgoing.at[placed].set(jnp.repeat(own_rows, top_count, axis=0))
    outgoing = outgoing.reshape(ep_count, tp_count, capacity, feature_width)
    arrived = lax.all_to_all(
        lax.all_to_all(outgoing, "ep", split_axis=0, concat_axis=0, tiled=True),
        "tp",
        split_axis=1,
        concat_axis=1,
        tiled=True,
    )
    computed = expert_apply(arrived, slot_gate_up, slot_down)
    returned = lax.all_to_all(
        lax.all_to_all(computed, "ep", split_axis=0, concat_axis=0, tiled=True),
        "tp",
        split_axis=1,
        concat_axis=1,
        tiled=True,
    )
    fetched = returned.reshape(-1, feature_width)[placed].reshape(quarter, top_count, feature_width)
    routed = jnp.einsum("qk,qkd->qd", gate_values, fetched, preferred_element_type=jnp.float32)
    own_partial = lax.dynamic_slice_in_dim(partial_value, row_start, quarter, 0) + routed
    partial_value = lax.dynamic_update_slice_in_dim(partial_value, own_partial, row_start, 0)
    summed = lax.psum_scatter(partial_value, "tp", scatter_dimension=1, tiled=True)
    live_rows = jnp.arange(tok_count, dtype=jnp.int32) < live_count[0]
    mixed_out = jnp.where(live_rows[:, None], hidden_in.astype(jnp.float32) + summed, 0.0)
    return mixed_out.astype(jnp.bfloat16)


def solution(mesh):
    in_specs = (
        P("ep", "tp"),
        P(),
        P(),
        P(None, None, "tp"),
        P("tp", None),
        P(("ep", "tp"), None, None, None),
        P(("ep", "tp"), None, None),
        P(),
        P("ep", None),
        P("ep"),
    )
    out_specs = P("ep", "tp")
    return jax.shard_map(local, mesh=mesh, in_specs=in_specs, out_specs=out_specs, check_vma=False)
```

profile of v0, /device:TPU:0, one launch (start us, length us, event | category | flops | bytes accessed | tf_op | source)
XLA Modules:
  0.0 238.2 jit_solution(8258291260687447549)
XLA Ops:
  6.5 9.0 %all_gather.3 = bf16[128,2048]{1,0:T(8,128)(2,1)S(1)} all-gather(bf16[128,512]{1,0:T(8,128)(2,1)} %param.10), channel_id=1, replica_groups=mesh['ep'=8,'tp'=4] {'tp'}, dimensions={1}, use_global_device_ids=true | all-gather | bytes 655360 | tf_op jit(solution)/shard_map/all_gather | solution.py:61
  19.2 2.2 reshape.86
  21.4 3.7 %scatter_custom_fusion = bf16[384,2048]{1,0:T(8,128)(2,1)} fusion(s32[192]{0:T(256)S(1)} %bitcast.43, bf16[192,2048]{1,0:T(8,128)(2,1)} %reshape.86, bf16[]{:T(256)} %constant.10.clone.1), kind=kCustom, calls=%fused_computation.14 | custom fusion | bytes 1573376 | tf_op jit(solution)/shard_map/scatter | solution.py:77
  25.1 3.6 %reshape.69 = bf16[8,4,12,2048]{3,2,1,0:T(8,128)(2,1)} reshape(bf16[384,2048]{1,0:T(8,128)(2,1)} %scatter_custom_fusion) | data formatting | bytes 3145728 | tf_op jit(solution)/shard_map/reshape | solution.py:78
  28.7 2.8 %copy.29 = bf16[8,4,12,2048]{3,1,2,0:T(4,128)(2,1)S(1)} copy(bf16[8,4,12,2048]{3,2,1,0:T(8,128)(2,1)} %reshape.69) | data formatting | bytes 3145728 | tf_op jit(solution)/shard_map/reshape | solution.py:78
  31.5 43.1 %all_to_all.20 = bf16[8,4,12,2048]{3,1,2,0:T(4,128)(2,1)S(1)} all-to-all(bf16[8,4,12,2048]{3,1,2,0:T(4,128)(2,1)S(1)} %copy.29), channel_id=1, replica_groups=mesh['ep'=8,'tp'=4] {'ep'}, dimensions={0} | all-to-all | bytes 3145728 | tf_op jit(solution)/shard_map/all_to_all | solution.py:80
  75.5 22.5 %all_to_all.21 = bf16[8,4,12,2048]{3,0,2,1:T(8,128)(2,1)S(1)} all-to-all(bf16[8,4,12,2048]{3,0,2,1:T(8,128)(2,1)S(1)} %copy.30), channel_id=1, replica_groups=mesh['ep'=8,'tp'=4] {'tp'}, dimensions={1} | all-to-all | bytes 3145728 | tf_op jit(solution)/shard_map/all_to_all | solution.py:79
  98.0 2.2 copy.31
  100.3 3.6 %reshape.91 = bf16[384,2048,1]{1,0,2:T(8,128)(2,1)} reshape(bf16[8,4,12,2048]{3,2,1,0:T(8,128)(2,1)} %copy.31) | data formatting | bytes 3145728 | tf_op jit(solution)/shard_map/reshape | solution.py:29
  103.9 5.6 %fusion = f32[384,2,704]{0,2,1:T(8,128)S(1)} fusion(bf16[384,2048,1]{1,0,2:T(8,128)(2,1)} %reshape.91, bf16[1,2048,2,704]{1,3,2,0:T(8,128)(2,1)} %param.15), kind=kOutput, calls=%fused_computation.2 | convolution fusion | flops 2214592512 | bytes 9502720 | tf_op jit(solution)/shard_map/rd,dgf->rgf/dot_general | solution.py:30
  109.5 2.6 %fusion.4 = bf16[384,2048]{1,0:T(8,128)(2,1)} fusion(bf16[1,704,2048]{2,1,0:T(8,128)(2,1)S(1)} %copy-done, f32[384,2,704]{0,2,1:T(8,128)S(1)} %fusion), kind=kOutput, calls=%fused_computation.6 | convolution fusion | flops 1109704704 | bytes 6619136 | tf_op jit(solution)/shard_map/dot_general | solution.py:34
  112.2 3.6 %reshape.71 = bf16[8,4,12,2048]{3,2,1,0:T(8,128)(2,1)} reshape(bf16[384,2048]{1,0:T(8,128)(2,1)} %fusion.4) | data formatting | bytes 3145728 | tf_op jit(solution)/shard_map/reshape | solution.py:37
  115.8 4.0 %copy.32 = bf16[8,4,12,2048]{3,1,2,0:T(4,128)(2,1)} copy(bf16[8,4,12,2048]{3,2,1,0:T(8,128)(2,1)} %reshape.71) | data formatting | bytes 3145728 | tf_op jit(solution)/shard_map/reshape | solution.py:37
  119.7 4.6 %all-to-all-start.2 = ((bf16[8,4,12,2048]{3,1,2,0:T(4,128)(2,1)}), bf16[8,4,12,2048]{3,1,2,0:T(4,128)(2,1)}, u32[]{:S(2)}, u32[]{:S(2)}) async-start(bf16[8,4,12,2048]{3,1,2,0:T(4,128)(2,1)} %copy.32), calls=%async_computation.2 | async-start | bytes 3145728 | tf_op jit(solution)/shard_map/all_to_all | solution.py:88
  124.5 36.6 %all-to-all-done.2 = bf16[8,4,12,2048]{3,1,2,0:T(4,128)(2,1)} async-done(((bf16[8,4,12,2048]{3,1,2,0:T(4,128)(2,1)}), bf16[8,4,12,2048]{3,1,2,0:T(4,128)(2,1)}, u32[]{:S(2)}, u32[]{:S(2)}) %all-to-all-start.2) | async-done | bytes 1572896 | tf_op jit(solution)/shard_map/all_to_all | solution.py:88
  161.1 3.4 %copy.33 = bf16[8,4,12,2048]{3,0,2,1:T(8,128)(2,1)} copy(bf16[8,4,12,2048]{3,1,2,0:T(4,128)(2,1)} %all-to-all-done.2) | data formatting | bytes 3145728 | tf_op jit(solution)/shard_map/all_to_all | solution.py:88
  164.5 4.5 %all-to-all-start.3 = ((bf16[8,4,12,2048]{3,0,2,1:T(8,128)(2,1)}), bf16[8,4,12,2048]{3,0,2,1:T(8,128)(2,1)}, u32[]{:S(2)}, u32[]{:S(2)}) async-start(bf16[8,4,12,2048]{3,0,2,1:T(8,128)(2,1)} %copy.33), calls=%async_computation.3 | async-start | bytes 3145728 | tf_op jit(solution)/shard_map/all_to_all | solution.py:87
  169.5 2.8 %fusion.15 = f32[128,2,352]{0,2,1:T(8,128)S(1)} fusion(bf16[2048,2,352]{0,2,1:T(8,128)(2,1)} %param.13, bf16[128,2048]{1,0:T(8,128)(2,1)S(1)} %copy-done.2), kind=kOutput, calls=%fused_computation.17 | convolution fusion | flops 369098752 | bytes 3768320 | tf_op jit(solution)/shard_map/td,dgf->tgf/dot_general | solution.py:65
  173.9 15.2 %all-to-all-done.3 = bf16[8,4,12,2048]{3,0,2,1:T(8,128)(2,1)} async-done(((bf16[8,4,12,2048]{3,0,2,1:T(8,128)(2,1)}), bf16[8,4,12,2048]{3,0,2,1:T(8,128)(2,1)}, u32[]{:S(2)}, u32[]{:S(2)}) %all-to-all-start.3) | async-done | bytes 1572896 | tf_op jit(solution)/shard_map/all_to_all | solution.py:87
  189.1 3.6 %copy.34 = bf16[8,4,12,2048]{3,2,1,0:T(8,128)(2,1)} copy(bf16[8,4,12,2048]{3,0,2,1:T(8,128)(2,1)} %all-to-all-done.3) | data formatting | bytes 3145728 | tf_op jit(solution)/shard_map/all_to_all | solution.py:87
  192.8 3.6 %reshape.72 = bf16[384,2048]{1,0:T(8,128)(2,1)} reshape(bf16[8,4,12,2048]{3,2,1,0:T(8,128)(2,1)} %copy.34) | data formatting | bytes 3145728 | tf_op jit(solution)/shard_map/reshape | solution.py:94
  196.4 4.4 %gather_fusion = bf16[192,2048]{1,0:T(8,128)(2,1)} fusion(bf16[384,2048]{1,0:T(8,128)(2,1)} %reshape.72, s32[1024]{0:T(1024)S(1)} %pad_clamp_fusion), kind=kCustom, calls=%fused_computation | custom fusion | bytes 1573632 | tf_op jit(solution)/shard_map/gather | solution.py:94
  200.8 2.2 reshape.73
  207.1 22.5 %reduce-scatter.2.cloned.1.call-done = f32[128,512]{1,0:T(8,128)} async-done(((f32[128,2048]{1,0:T(8,128)}), f32[128,512]{1,0:T(8,128)}) %reduce-scatter.2.cloned.1.call-update) | async-done | bytes 262160 | tf_op jit(solution)/shard_map/reduce_scatter | solution.py:98
  (44 shorter events, 11.8 us)
Async XLA Ops:
  6.5 103.0 %copy-start = (bf16[1,704,2048]{2,1,0:T(8,128)(2,1)S(1)}, bf16[1,704,2048]{2,1,0:T(8,128)(2,1)}, u32[]{:S(2)}) copy-start(bf16[1,704,2048]{2,1,0:T(8,128)(2,1)} %param.16) | copy-start | bytes 8650756
  6.5 10.9 %copy-start.6 = (s32[128,6]{0,1:T(8,128)S(1)}, s32[128,6]{0,1:T(8,128)}, u32[]{:S(2)}) copy-start(s32[128,6]{0,1:T(8,128)} %param.18) | copy-start | bytes 9220
  16.6 0.8 copy-start.1
  119.7 4.6 %copy-start.5 = (bf16[2048,8]{0,1:T(8,128)(2,1)S(1)}, bf16[2048,8]{0,1:T(8,128)(2,1)}, u32[]{:S(2)}) copy-start(bf16[2048,8]{0,1:T(8,128)(2,1)} %param.12) | copy-start | bytes 98308
  119.7 41.3 %all-to-all-start.2 = ((bf16[8,4,12,2048]{3,1,2,0:T(4,128)(2,1)}), bf16[8,4,12,2048]{3,1,2,0:T(4,128)(2,1)}, u32[]{:S(2)}, u32[]{:S(2)}) async-start(bf16[8,4,12,2048]{3,1,2,0:T(4,128)(2,1)} %copy.32), calls=%async_computation.2 | async-start | bytes 3145728 | tf_op jit(solution)/shard_map/all_to_all | solution.py:88
  164.5 4.5 %copy-start.7 = (s32[32]{0:T(128)S(1)}, s32[32]{0:T(128)}, u32[]{:S(2)}) copy-start(s32[32]{0:T(128)} %param.17) | copy-start | bytes 388
  164.5 5.0 %copy-start.2 = (bf16[128,2048]{1,0:T(8,128)(2,1)S(1)}, bf16[128,2048]{1,0:T(8,128)(2,1)}, u32[]{:S(2)}) copy-start(bf16[128,2048]{1,0:T(8,128)(2,1)} %copy-done.1) | copy-start | bytes 1572868
  164.5 24.6 %all-to-all-start.3 = ((bf16[8,4,12,2048]{3,0,2,1:T(8,128)(2,1)}), bf16[8,4,12,2048]{3,0,2,1:T(8,128)(2,1)}, u32[]{:S(2)}, u32[]{:S(2)}) async-start(bf16[8,4,12,2048]{3,0,2,1:T(8,128)(2,1)} %copy.33), calls=%async_computation.3 | async-start | bytes 3145728 | tf_op jit(solution)/shard_map/all_to_all | solution.py:87
  169.0 60.6 %reduce-scatter.2.cloned.1.call-start = ((), (), s32[]{:S(2)}) async-start(), calls=%async_computation.5 | async-start | bytes 1310720 | tf_op jit(solution)/shard_map/reduce_scatter | solution.py:98
  169.5 2.9 %copy-start.3 = (bf16[352,2048]{1,0:T(8,128)(2,1)S(1)}, bf16[352,2048]{1,0:T(8,128)(2,1)}, u32[]{:S(2)}) copy-start(bf16[352,2048]{1,0:T(8,128)(2,1)} %param.14) | copy-start | bytes 4325380
  203.0 26.6 %copy-start.4 = (bf16[128,512]{1,0:T(8,128)(2,1)S(1)}, bf16[128,512]{1,0:T(8,128)(2,1)}, u32[]{:S(2)}) copy-start(bf16[128,512]{1,0:T(8,128)(2,1)} %param.10) | copy-start | bytes 393220
Sparse Core Ops, SparseCore 0:
  206.6 22.9 reduce-scatter.1
where the time goes:
time: 239 us; the launch traced here: 238 us
  blocking collectives  74.6 us (31%)
  waiting for transfers between devices  74.3 us (31%)
  local copies, waits for them, and re-layouts  46.3 us (19%)
  matrix products  14.5 us (6%)
  between operations  14.2 us (6%)
  starting transfers between devices  9.12 us (4%)
  other arithmetic  5.13 us (2%)
    all_to_all x1, blocking collectives, local(): lax.all_to_all(outgoing, 'ep', split_axis=0, concat_axis=0, tiled=True)  43.1 us
    all_to_all x1, waiting for transfers between devices, local(): lax.all_to_all(computed, 'ep', split_axis=0, concat_axis=0, tiled=True)  36.6 us
    all_to_all x1, blocking collectives, local(): lax.all_to_all(lax.all_to_all(outgoing, 'ep', split_axis=0, concat_axis=0...  22.5 us
    reduce_scatter x1, waiting for transfers between devices, local(): lax.psum_scatter(partial_value, 'tp', scatter_dimension=1, tiled=True)  22.5 us
    all_to_all x1, waiting for transfers between devices, local(): lax.all_to_all(lax.all_to_all(computed, 'ep', split_axis=0, concat_axis=0...  15.2 us
    all_gather x1, blocking collectives, local(): full_rows = lax.all_gather(hidden_in, 'tp', axis=1, tiled=True)  8.98 us
    reshape x2, local copies, waits for them, and re-layouts, expert_apply(): return result.reshape(shape_in)  7.55 us
    reshape x2, local copies, waits for them, and re-layouts, local(): outgoing = outgoing.reshape(ep_count, tp_count, capacity, feature_width)  6.42 us
  transfers between devices with their start and end apart: 3, of which 3 were waited for; matrix products, arithmetic and copies ran while one was open for 2% of the time, Pallas kernels for 0%

commit v1 on v0

--- a/solution.py
+++ b/solution.py
@@ -76,13 +76,11 @@
     outgoing = jnp.zeros((slot_count * capacity, feature_width), jnp.bfloat16)
     outgoing = outgoing.at[placed].set(jnp.repeat(own_rows, top_count, axis=0))
     outgoing = outgoing.reshape(ep_count, tp_count, capacity, feature_width)
-    arrived = lax.all_to_all(
-        lax.all_to_all(outgoing, "ep", split_axis=0, concat_axis=0, tiled=True),
-        "tp",
-        split_axis=1,
-        concat_axis=1,
-        tiled=True,
-    )
+    block = lax.all_to_all(outgoing, "ep", split_axis=0, concat_axis=0, tiled=True)
+    size = lax.axis_size("tp")
+    pieces = jnp.stack(jnp.split(block, size, axis=1), axis=0)
+    pieces = lax.all_to_all(pieces, "tp", split_axis=0, concat_axis=0)
+    arrived = jnp.concatenate(pieces, axis=1)
     computed = expert_apply(arrived, slot_gate_up, slot_down)
     returned = lax.all_to_all(
         lax.all_to_all(computed, "ep", split_axis=0, concat_axis=0, tiled=True),

time: 239 us -> 243 us (1.017)
  local copies, waits for them, and re-layouts: 46.3 us -> 49.3 us
    another operation x0 -> x3, local copies, waits for them, and re-layouts: none -> 5.3 us  [the longest x1 3.61 us: expert_apply(): flat_rows = received.reshape(-1, shape_in[-1])]
    all_to_all x2 -> x0, local copies, waits for them, and re-layouts: 3.1 us -> none  [the longest x1 2.24 us: local(): lax.all_to_all(lax.all_to_all(outgoing, 'ep', split_axis=0, concat_axis=0...]
    split x0 -> x1, local copies, waits for them, and re-layouts: none -> 2.92 us  [local(): pieces = jnp.stack(jnp.split(block, size, axis=1), axis=0)]
where the time goes in v1:
time: 243 us; the launch traced here: 242 us
  blocking collectives  74.5 us (31%)
  waiting for transfers between devices  73.8 us (30%)
  local copies, waits for them, and re-layouts  49.3 us (20%)
  matrix products  15.2 us (6%)
  between operations  14.2 us (6%)
  starting transfers between devices  8.82 us (4%)
  other arithmetic  6.16 us (3%)
    all_to_all x1, blocking collectives, local(): lax.all_to_all(outgoing, 'ep', split_axis=0, concat_axis=0, tiled=True)  43.1 us
    all_to_all x1, waiting for transfers between devices, local(): lax.all_to_all(computed, 'ep', split_axis=0, concat_axis=0, tiled=True)  36 us
    all_to_all x1, blocking collectives, local(): pieces = lax.all_to_all(pieces, 'tp', split_axis=0, concat_axis=0)  22.5 us
    reduce_scatter x1, waiting for transfers between devices, local(): lax.psum_scatter(partial_value, 'tp', scatter_dimension=1, tiled=True)  22.5 us
    all_to_all x1, waiting for transfers between devices, local(): lax.all_to_all(lax.all_to_all(computed, 'ep', split_axis=0, concat_axis=0...  15.3 us
    all_gather x1, blocking collectives, local(): full_rows = lax.all_gather(hidden_in, 'tp', axis=1, tiled=True)  8.86 us
    reshape x2, local copies, waits for them, and re-layouts, expert_apply(): return result.reshape(shape_in)  7.57 us
    reshape x2, local copies, waits for them, and re-layouts, local(): outgoing = outgoing.reshape(ep_count, tp_count, capacity, feature_width)  6.43 us
  transfers between devices with their start and end apart: 3, of which 3 were waited for; matrix products, arithmetic and copies ran while one was open for 2% of the time, Pallas kernels for 0%

profile of v1, /device:TPU:0, one launch (start us, length us, event | category | flops | bytes accessed | tf_op | source)
XLA Modules:
  0.0 242.0 jit_solution(12542555993099882972)
XLA Ops:
  8.0 8.9 %all_gather.3 = bf16[128,2048]{1,0:T(8,128)(2,1)S(1)} all-gather(bf16[128,512]{1,0:T(8,128)(2,1)} %param.10), channel_id=1, replica_groups=mesh['ep'=8,'tp'=4] {'tp'}, dimensions={1}, use_global_device_ids=true | all-gather | bytes 655360 | tf_op jit(solution)/shard_map/all_gather | solution.py:61
  21.3 3.7 %scatter_custom_fusion = bf16[384,2048]{1,0:T(8,128)(2,1)} fusion(s32[192]{0:T(256)S(1)} %bitcast.55, bf16[192,2048]{1,0:T(8,128)(2,1)} %reshape.86, bf16[]{:T(256)} %constant.10.clone.1), kind=kCustom, calls=%fused_computation.15 | custom fusion | bytes 1573376 | tf_op jit(solution)/shard_map/scatter | solution.py:77
  25.0 3.6 %reshape.69 = bf16[8,4,12,2048]{3,2,1,0:T(8,128)(2,1)} reshape(bf16[384,2048]{1,0:T(8,128)(2,1)} %scatter_custom_fusion) | data formatting | bytes 3145728 | tf_op jit(solution)/shard_map/reshape | solution.py:78
  28.6 2.8 %copy.52 = bf16[8,4,12,2048]{3,1,2,0:T(4,128)(2,1)S(1)} copy(bf16[8,4,12,2048]{3,2,1,0:T(8,128)(2,1)} %reshape.69) | data formatting | bytes 3145728 | tf_op jit(solution)/shard_map/reshape | solution.py:78
  31.5 43.1 %all_to_all.20 = bf16[8,4,12,2048]{3,1,2,0:T(4,128)(2,1)S(1)} all-to-all(bf16[8,4,12,2048]{3,1,2,0:T(4,128)(2,1)S(1)} %copy.52), channel_id=1, replica_groups=mesh['ep'=8,'tp'=4] {'ep'}, dimensions={0} | all-to-all | bytes 3145728 | tf_op jit(solution)/shard_map/all_to_all | solution.py:79
  74.5 2.9 %fusion.28 = (bf16[8,1,12,2048]{3,1,2,0:T(2,128)(2,1)S(1)}, bf16[8,1,12,2048]{3,1,2,0:T(2,128)(2,1)S(1)}, bf16[8,1,12,2048]{3,1,2,0:T(2,128)(2,1)S(1)}, bf16[8,1,12,2048]{3,1,2,0:T(2,128)(2,1)S(1)}) fusion(bf16[8,4,12,2048]{3,1,2,0:T(4,128)(2,1)S(1)} %all_to_all.20), kind=kLoop, calls=%fused_computation.53 | loop fusion | bytes 3145728 | tf_op jit(solution)/shard_map/split | solution.py:81
  79.4 22.5 %all_to_all.21 = bf16[4,8,1,12,2048]{4,1,3,2,0:T(8,128)(2,1)S(1)} all-to-all(bf16[4,8,1,12,2048]{4,1,3,2,0:T(8,128)(2,1)S(1)} %pad_maximum_fusion), channel_id=1, replica_groups=mesh['ep'=8,'tp'=4] {'tp'}, dimensions={0} | all-to-all | bytes 3145728 | tf_op jit(solution)/shard_map/all_to_all | solution.py:82
  101.9 2.2 copy.57
  104.1 3.6 %reshape.91 = bf16[384,2048,1]{1,0,2:T(8,128)(2,1)} reshape(bf16[8,4,1,12,2048]{4,3,1,0,2:T(8,128)(2,1)} %copy.57) | data formatting | bytes 3145728 | tf_op jit(solution)/shard_map/reshape;reshape | solution.py:29
  107.7 5.6 %fusion = f32[384,2,704]{0,2,1:T(8,128)S(1)} fusion(bf16[384,2048,1]{1,0,2:T(8,128)(2,1)} %reshape.91, bf16[1,2048,2,704]{1,3,2,0:T(8,128)(2,1)} %param.15), kind=kOutput, calls=%fused_computation.2 | convolution fusion | flops 2214592512 | bytes 9502720 | tf_op jit(solution)/shard_map/rd,dgf->rgf/dot_general | solution.py:30
  113.4 2.7 %fusion.4 = bf16[384,2048]{1,0:T(8,128)(2,1)} fusion(bf16[1,704,2048]{2,1,0:T(8,128)(2,1)S(1)} %copy-done, f32[384,2,704]{0,2,1:T(8,128)S(1)} %fusion), kind=kOutput, calls=%fused_computation.6 | convolution fusion | flops 1109704704 | bytes 6619136 | tf_op jit(solution)/shard_map/dot_general | solution.py:34
  116.1 3.6 %reshape.71 = bf16[8,4,12,2048]{3,2,1,0:T(8,128)(2,1)} reshape(bf16[384,2048]{1,0:T(8,128)(2,1)} %fusion.4) | data formatting | bytes 3145728 | tf_op jit(solution)/shard_map/reshape | solution.py:37
  119.7 4.0 %copy.58 = bf16[8,4,12,2048]{3,1,2,0:T(4,128)(2,1)} copy(bf16[8,4,12,2048]{3,2,1,0:T(8,128)(2,1)} %reshape.71) | data formatting | bytes 3145728 | tf_op jit(solution)/shard_map/reshape | solution.py:37
  123.6 4.3 %all-to-all-start.2 = ((bf16[8,4,12,2048]{3,1,2,0:T(4,128)(2,1)}), bf16[8,4,12,2048]{3,1,2,0:T(4,128)(2,1)}, u32[]{:S(2)}, u32[]{:S(2)}) async-start(bf16[8,4,12,2048]{3,1,2,0:T(4,128)(2,1)} %copy.58), calls=%async_computation.2 | async-start | bytes 3145728 | tf_op jit(solution)/shard_map/all_to_all | solution.py:86
  128.8 36.0 %all-to-all-done.2 = bf16[8,4,12,2048]{3,1,2,0:T(4,128)(2,1)} async-done(((bf16[8,4,12,2048]{3,1,2,0:T(4,128)(2,1)}), bf16[8,4,12,2048]{3,1,2,0:T(4,128)(2,1)}, u32[]{:S(2)}, u32[]{:S(2)}) %all-to-all-start.2) | async-done | bytes 1572896 | tf_op jit(solution)/shard_map/all_to_all | solution.py:86
  164.9 3.4 %copy.59 = bf16[8,4,12,2048]{3,0,2,1:T(8,128)(2,1)} copy(bf16[8,4,12,2048]{3,1,2,0:T(4,128)(2,1)} %all-to-all-done.2) | data formatting | bytes 3145728 | tf_op jit(solution)/shard_map/all_to_all | solution.py:86
  168.3 4.5 %all-to-all-start.3 = ((bf16[8,4,12,2048]{3,0,2,1:T(8,128)(2,1)}), bf16[8,4,12,2048]{3,0,2,1:T(8,128)(2,1)}, u32[]{:S(2)}, u32[]{:S(2)}) async-start(bf16[8,4,12,2048]{3,0,2,1:T(8,128)(2,1)} %copy.59), calls=%async_computation.3 | async-start | bytes 3145728 | tf_op jit(solution)/shard_map/all_to_all | solution.py:85
  173.3 2.8 %fusion.15 = f32[128,2,352]{0,2,1:T(8,128)S(1)} fusion(bf16[2048,2,352]{0,2,1:T(8,128)(2,1)} %param.13, bf16[128,2048]{1,0:T(8,128)(2,1)S(1)} %fusion.10), kind=kOutput, calls=%fused_computation.18 | convolution fusion | flops 369098752 | bytes 3768320 | tf_op jit(solution)/shard_map/td,dgf->tgf/dot_general | solution.py:65
  177.6 15.3 %all-to-all-done.3 = bf16[8,4,12,2048]{3,0,2,1:T(8,128)(2,1)} async-done(((bf16[8,4,12,2048]{3,0,2,1:T(8,128)(2,1)}), bf16[8,4,12,2048]{3,0,2,1:T(8,128)(2,1)}, u32[]{:S(2)}, u32[]{:S(2)}) %all-to-all-start.3) | async-done | bytes 1572896 | tf_op jit(solution)/shard_map/all_to_all | solution.py:85
  192.9 3.7 %copy.60 = bf16[8,4,12,2048]{3,2,1,0:T(8,128)(2,1)} copy(bf16[8,4,12,2048]{3,0,2,1:T(8,128)(2,1)} %all-to-all-done.3) | data formatting | bytes 3145728 | tf_op jit(solution)/shard_map/all_to_all | solution.py:85
  196.6 3.6 %reshape.72 = bf16[384,2048]{1,0:T(8,128)(2,1)} reshape(bf16[8,4,12,2048]{3,2,1,0:T(8,128)(2,1)} %copy.60) | data formatting | bytes 3145728 | tf_op jit(solution)/shard_map/reshape | solution.py:92
  200.2 4.4 %gather_fusion = bf16[192,2048]{1,0:T(8,128)(2,1)} fusion(bf16[384,2048]{1,0:T(8,128)(2,1)} %reshape.72, s32[1024]{0:T(1024)S(1)} %pad_clamp_fusion), kind=kCustom, calls=%fused_computation | custom fusion | bytes 1573632 | tf_op jit(solution)/shard_map/gather | solution.py:92
  204.6 2.2 reshape.73
  210.9 22.5 %reduce-scatter.2.cloned.1.call-done = f32[128,512]{1,0:T(8,128)} async-done(((f32[128,2048]{1,0:T(8,128)}), f32[128,512]{1,0:T(8,128)}) %reduce-scatter.2.cloned.1.call-update) | async-done | bytes 262160 | tf_op jit(solution)/shard_map/reduce_scatter | solution.py:96
  (39 shorter events, 15.8 us)
Async XLA Ops:
  6.5 106.9 %copy-start = (bf16[1,704,2048]{2,1,0:T(8,128)(2,1)S(1)}, bf16[1,704,2048]{2,1,0:T(8,128)(2,1)}, u32[]{:S(2)}) copy-start(bf16[1,704,2048]{2,1,0:T(8,128)(2,1)} %param.16) | copy-start | bytes 8650756
  123.6 41.2 %all-to-all-start.2 = ((bf16[8,4,12,2048]{3,1,2,0:T(4,128)(2,1)}), bf16[8,4,12,2048]{3,1,2,0:T(4,128)(2,1)}, u32[]{:S(2)}, u32[]{:S(2)}) async-start(bf16[8,4,12,2048]{3,1,2,0:T(4,128)(2,1)} %copy.58), calls=%async_computation.2 | async-start | bytes 3145728 | tf_op jit(solution)/shard_map/all_to_all | solution.py:86
  168.3 4.6 %copy-start.3 = (s32[32]{0:T(128)S(1)}, s32[32]{0:T(128)}, u32[]{:S(2)}) copy-start(s32[32]{0:T(128)} %param.17) | copy-start | bytes 388
  168.3 24.6 %all-to-all-start.3 = ((bf16[8,4,12,2048]{3,0,2,1:T(8,128)(2,1)}), bf16[8,4,12,2048]{3,0,2,1:T(8,128)(2,1)}, u32[]{:S(2)}, u32[]{:S(2)}) async-start(bf16[8,4,12,2048]{3,0,2,1:T(8,128)(2,1)} %copy.59), calls=%async_computation.3 | async-start | bytes 3145728 | tf_op jit(solution)/shard_map/all_to_all | solution.py:85
  172.8 60.7 %reduce-scatter.2.cloned.1.call-start = ((), (), s32[]{:S(2)}) async-start(), calls=%async_computation.5 | async-start | bytes 1310720 | tf_op jit(solution)/shard_map/reduce_scatter | solution.py:96
  173.3 2.9 %copy-start.1 = (bf16[352,2048]{1,0:T(8,128)(2,1)S(1)}, bf16[352,2048]{1,0:T(8,128)(2,1)}, u32[]{:S(2)}) copy-start(bf16[352,2048]{1,0:T(8,128)(2,1)} %param.14) | copy-start | bytes 4325380
  206.8 26.6 %copy-start.2 = (bf16[128,512]{1,0:T(8,128)(2,1)S(1)}, bf16[128,512]{1,0:T(8,128)(2,1)}, u32[]{:S(2)}) copy-start(bf16[128,512]{1,0:T(8,128)(2,1)} %param.10) | copy-start | bytes 393220
Sparse Core Ops, SparseCore 0:
  210.4 23.0 reduce-scatter.1
